TPU v7x, 128 devices: a whole 4x4x4 slice. The times are simulated.
128 devices in a mesh: pipe: 8 (over y, x_lo), seq: 16 (over z, x_hi, core).
Axes of the slice: x: 4 (x_hi: 2, x_lo: 2; x = x_hi * 2 + x_lo), y: 4, z: 4, core: 2. Of those that a mesh axis runs over, the one named last changes fastest.
Arguments:
- held: bfloat16 [8, 2048, 1536], P('pipe', 'seq'), may hold values from -6 to 6
- entering: bfloat16 [2048, 1536], P('seq'), may hold values from -6 to 6
- counts: int32 [9], replicated, may hold values from 1 to 256
- kind: int32 [8], P('pipe'), may hold values from 0 to 1
- modulation: float32 [8, 6, 1536], P('pipe'), may hold values from -4 to 4
- w_qkv: bfloat16 [8, 1536, 6144], P('pipe'), may hold values from -0.15625 to 0.15625
- w_out: bfloat16 [8, 2048, 1536], P('pipe'), may hold values from -0.125 to 0.125
- q_gain: float32 [8, 128], P('pipe'), may hold values from 1.5 to 6
- k_gain: float32 [8, 128], P('pipe'), may hold values from 1.5 to 6
Outputs:
- arrived: bfloat16 [2, 8, 2048, 1536], P(None, 'pipe', 'seq')
All inputs are finite; a program needn't handle non-finite values.
Results may differ from a plain program's by a relative error of at most 0.023.
The roundings to bfloat16 on the way count: a program that leaves them out, or rounds other values in their place, can miss the bound.
Values may be sent and summed in bfloat16 or wider, within the bound.
A program may use at most 128 MiB of HBM per device.

v0:
```python
import jax
import jax.numpy as jnp
from jax import lax
from jax.sharding import PartitionSpec as P

HD = 128
TXT = 256
eps = 1e-06


def from_behind(value, axis, steps):
    count = lax.axis_size(axis)
    pairs = [(source, (source + steps) % count) for source in range(count)]
    return lax.ppermute(value, axis, pairs)


def rms_heads(values_f32, gain):
    return (
        values_f32
        * lax.rsqrt(jnp.mean(values_f32 * values_f32, axis=-1, keepdims=True) + eps)
        * gain
    )


def shards(held, entering, counts, kind, modulation, w_qkv, w_out, q_gain, k_gain):
    section_id = lax.axis_index("pipe")
    seq_rank = lax.axis_index("seq")
    seq_devices = lax.axis_size("seq")
    tok_rows = held.shape[1]
    seq_total = tok_rows * seq_devices
    text_start = seq_total - TXT
    inner_width = w_out.shape[1]
    head_count = inner_width // HD
    section_count = counts.shape[0] - 1
    positions = seq_rank * tok_rows + jnp.arange(tok_rows, dtype=jnp.int32)
    params = modulation[0]
    choose = ((positions >= text_start) & (kind[0] == 0))[:, None]
    shift_row = jnp.where(choose, params[3], params[0])
    scale_row = jnp.where(choose, params[4], params[1])
    gate_row = jnp.where(choose, params[5], params[2])
    factor_scale = HD ** (-0.5)

    def pass_on(outcome):
        return from_behind(outcome, "pipe", 1)

    def run_block(resid, text_live):
        resid_f32 = resid.astype(jnp.float32)
        center = resid_f32 - jnp.mean(resid_f32, axis=-1, keepdims=True)
        normed = center * lax.rsqrt(jnp.mean(center * center, axis=-1, keepdims=True) + eps)
        mixed_in = (normed * (1.0 + scale_row) + shift_row).astype(jnp.bfloat16)
        projected = jnp.dot(mixed_in, w_qkv[0], preferred_element_type=jnp.float32)
        query_heads = rms_heads(
            projected[:, :inner_width].reshape(tok_rows, head_count, HD), q_gain[0]
        ).astype(jnp.bfloat16)
        key_heads = rms_heads(
            projected[:, inner_width : 2 * inner_width].reshape(tok_rows, head_count, HD), k_gain[0]
        ).astype(jnp.bfloat16)
        value_heads = (
            projected[:, 2 * inner_width :].reshape(tok_rows, head_count, HD).astype(jnp.bfloat16)
        )
        key_limit = text_start + text_live
        row_top = jnp.full((head_count, tok_rows), -1e30, jnp.float32)
        key_piece = lax.all_gather(key_heads, "seq", axis=0, tiled=True)
        value_piece = lax.all_gather(value_heads, "seq", axis=0, tiled=True)
        scores = (
            jnp.einsum("qhd,khd->hqk", query_heads, key_piece, preferred_element_type=jnp.float32)
            * factor_scale
        )
        key_pos = jnp.arange(key_piece.shape[0], dtype=jnp.int32)
        scores = jnp.where((key_pos < key_limit)[None, None, :], scores, -1e30)
        new_top = jnp.maximum(row_top, jnp.max(scores, axis=-1))
        weights = jnp.exp(scores - new_top[..., None])
        denom = jnp.sum(weights, axis=-1)
        accum = jnp.einsum(
            "hqk,khd->hqd",
            weights.astype(jnp.bfloat16),
            value_piece,
            preferred_element_type=jnp.float32,
        )
        row_top, denom, accum = (new_top, denom, accum)
        attended = (accum / denom[..., None]).astype(jnp.bfloat16).transpose(1, 0, 2)
        merged = attended.reshape(tok_rows, inner_width)
        update = jnp.dot(merged, w_out[0], preferred_element_type=jnp.float32)
        return (resid_f32 + gate_row * update).astype(jnp.bfloat16)

    outcome_one = run_block(held[0], counts[section_id])
    arrived_one = pass_on(outcome_one)
    inputs_two = jnp.where(section_id == 0, entering, arrived_one)
    outcome_two = run_block(inputs_two, counts[(section_id + section_count) % (section_count + 1)])
    arrived_two = pass_on(outcome_two)
    return jnp.stack([arrived_one, arrived_two])[:, None]


def solution(mesh):
    placed = (
        P("pipe", "seq", None),
        P("seq", None),
        P(),
        P("pipe"),
        P("pipe", None, None),
        P("pipe", None, None),
        P("pipe", None, None),
        P("pipe", None),
        P("pipe", None),
    )
    return jax.shard_map(
        shards, mesh=mesh, in_specs=placed, out_specs=P(None, "pipe", "seq", None), check_vma=False
    )
```

profile of v0, /device:TPU:1, one launch (start us, length us, event | category | flops | bytes accessed | tf_op | source)
XLA Modules:
  0.0 398.3 jit_solution(795105245037220855)
XLA Ops:
  6.5 0.9 slice_reduce_fusion.5
  8.1 1.1 convert_reduce_fusion.1
  9.2 1.2 fusion.64
  10.6 8.1 %fusion.2 = f32[128,6144]{1,0:T(8,128)S(1)} fusion(bf16[1,1536,6144]{2,1,0:T(8,128)(2,1)} %param.14, bf16[1,128,1536]{2,1,0:T(8,128)(2,1)} %param.9, f32[1536]{0:T(1024)S(1)} %get-tuple-element.9, f32[1536]{0:T(1024)S(1)} %get-tuple-element.10, f32[1536]{0:T(1024)S(1)} %get-tuple-element.6, f32[1536]{0:T(1024)S(1)} %get-tuple-element.7, ...), kind=kOutput, calls=%fused_computation.2 | convolution fusion | flops 2417688576 | bytes 22439040 | tf_op jit(solution)/shard_map/dot_general | solution.py:51
  18.7 1.6 slice_bitcast_fusion.1
  20.4 0.2 copy.62
  20.6 0.3 multiply_reduce_fusion.2
  20.9 0.1 copy.47
  21.0 2.4 fusion.51
  23.4 0.9 slice.75
  24.3 2.0 copy.58
  26.4 1.4 copy.61
  27.8 0.3 multiply_reduce_fusion.3
  28.3 0.1 copy.46
  28.4 0.6 fusion.98
  29.7 0.3 multiply_convert_fusion.2
  30.0 70.0 %all-gather.5.cloned.1.call-done = bf16[2048,16,128]{2,0,1:T(8,128)(2,1)} async-done(((bf16[128,16,128]{2,0,1:T(8,128)(2,1)}), bf16[2048,16,128]{2,0,1:T(8,128)(2,1)}) %all-gather.5.cloned.1.call-update) | async-done | bytes 8388624 | tf_op jit(solution)/shard_map/all_gather | solution.py:63
  100.0 12.1 %fusion.4 = (f32[16,128]{1,0:T(8,128)S(1)}, f32[16,128,2048]{2,1,0:T(8,128)}) fusion(pred[2048]{0:T(1024)(128)(4,1)S(1)} %iota_compare_fusion.1, bf16[2048,16,128]{2,0,1:T(8,128)(2,1)} %all-gather.5.cloned.1.call-done, bf16[128,16,128]{2,1,0:T(8,128)(2,1)S(1)} %multiply_convert_fusion.2), kind=kOutput, calls=%fused_computation.8 | convolution fusion | flops 1086322688 | bytes 25700352 | tf_op jit(solution)/shard_map/qhd,khd->hqk/dot_general | solution.py:66
  112.1 7.9 %fusion.6 = f32[16,128]{1,0:T(8,128)S(1)} fusion(f32[16,128,2048]{2,1,0:T(8,128)} %get-tuple-element.21, f32[16,128]{1,0:T(8,128)S(1)} %broadcast_maximum_fusion.1, pred[2048]{0:T(1024)(128)(4,1)S(1)} %iota_compare_fusion.1), kind=kLoop, calls=%fused_computation.10 | loop fusion | flops 16775168 | bytes 16795648 | tf_op jit(solution)/shard_map/reduce_sum | solution.py:73
  120.0 56.6 %all-gather.7.cloned.1.call-done = bf16[2048,16,128]{0,2,1:T(8,128)(2,1)} async-done(((bf16[128,16,128]{0,2,1:T(8,128)(2,1)}), bf16[2048,16,128]{0,2,1:T(8,128)(2,1)}) %all-gather.7.cloned.1.call-update) | async-done | bytes 8388624 | tf_op jit(solution)/shard_map/all_gather | solution.py:64
  176.6 10.7 %divide_convert_fusion.1 = bf16[128,16,128]{0,2,1:T(8,128)(2,1)S(1)} fusion(bf16[2048,16,128]{0,2,1:T(8,128)(2,1)} %all-gather.7.cloned.1.call-done, f32[16,128,2048]{2,1,0:T(8,128)} %get-tuple-element.21, f32[16,128]{1,0:T(8,128)S(1)} %broadcast_maximum_fusion.1, pred[2048]{0:T(1024)(128)(4,1)S(1)} %iota_compare_fusion.1, f32[128,16]{0,1:T(8,128)S(1)} %bitcast.101), kind=kOutput, calls=%fused_computation.53 | convolution fusion | flops 1091043328 | bytes 25708544 | tf_op jit(solution)/shard_map/hqk,khd->hqd/dot_general | solution.py:74
  187.4 1.0 fusion.41
  188.5 0.5 collective-permute-start
  189.0 12.2 %collective-permute-done = bf16[128,1536]{1,0:T(8,128)(2,1)S(1)} collective-permute-done((bf16[128,1536]{1,0:T(8,128)(2,1)S(1)}, bf16[128,1536]{1,0:T(8,128)(2,1)S(1)}, u32[]{:S(2)}, u32[]{:S(2)}) %collective-permute-start) | collective-permute-done | bytes 393248 | tf_op jit(solution)/shard_map/ppermute | solution.py:14
  201.2 0.2 convert_reduce_fusion
  201.4 0.3 fusion.59
  201.7 0.3 copy-done.1
  202.0 8.1 %fusion = f32[128,6144]{1,0:T(8,128)S(1)} fusion(bf16[1,1536,6144]{2,1,0:T(8,128)(2,1)} %param.14, bf16[128,1536]{1,0:T(8,128)(2,1)S(1)} %get-tuple-element.12, f32[1536]{0:T(1024)} %copy-done.4, f32[1536]{0:T(1024)} %copy-done.5, f32[1536]{0:T(1024)S(1)} %get-tuple-element.6, f32[1536]{0:T(1024)S(1)} %get-tuple-element.7, f32[128]{0:T(128)S(1)} %add_rsqrt_fusion.4, ...), kind=kOutput, calls=%fused_computation | convolution fusion | flops 2417688576 | bytes 22439040 | tf_op jit(solution)/shard_map/dot_general | solution.py:51
  210.1 1.5 slice_bitcast_fusion
  211.6 2.5 copy.53
  214.1 1.3 multiply_reduce_fusion
  215.4 2.6 copy.54
  218.0 2.4 multiply_convert_fusion
  220.5 0.9 slice.74
  221.3 2.0 copy.59
  224.0 1.4 copy.63
  225.4 0.3 multiply_reduce_fusion.1
  225.8 0.1 copy.52
  225.9 0.3 multiply_convert_fusion.1
  226.3 63.6 %all-gather.9.cloned.1.call-done = bf16[2048,16,128]{2,0,1:T(8,128)(2,1)} async-done(((bf16[128,16,128]{2,0,1:T(8,128)(2,1)}), bf16[2048,16,128]{2,0,1:T(8,128)(2,1)}) %all-gather.9.cloned.1.call-update) | async-done | bytes 8388624 | tf_op jit(solution)/shard_map/all_gather | solution.py:63
  289.9 12.1 %fusion.5 = (f32[16,128]{1,0:T(8,128)S(1)}, f32[16,128,2048]{2,1,0:T(8,128)}) fusion(pred[2048]{0:T(1024)(128)(4,1)S(1)} %iota_compare_fusion, bf16[2048,16,128]{2,0,1:T(8,128)(2,1)} %all-gather.9.cloned.1.call-done, bf16[128,16,128]{2,1,0:T(8,128)(2,1)S(1)} %multiply_convert_fusion.1), kind=kOutput, calls=%fused_computation.9 | convolution fusion | flops 1086322688 | bytes 25700352 | tf_op jit(solution)/shard_map/qhd,khd->hqk/dot_general | solution.py:66
  302.0 7.9 %fusion.8 = f32[16,128]{1,0:T(8,128)S(1)} fusion(f32[16,128,2048]{2,1,0:T(8,128)} %get-tuple-element.23, f32[16,128]{1,0:T(8,128)S(1)} %broadcast_maximum_fusion, pred[2048]{0:T(1024)(128)(4,1)S(1)} %iota_compare_fusion), kind=kLoop, calls=%fused_computation.12 | loop fusion | flops 16775168 | bytes 16795648 | tf_op jit(solution)/shard_map/reduce_sum | solution.py:73
  309.9 56.4 %all-gather.11.cloned.1.call-done = bf16[2048,16,128]{0,2,1:T(8,128)(2,1)} async-done(((bf16[128,16,128]{0,2,1:T(8,128)(2,1)}), bf16[2048,16,128]{0,2,1:T(8,128)(2,1)}) %all-gather.11.cloned.1.call-update) | async-done | bytes 8388624 | tf_op jit(solution)/shard_map/all_gather | solution.py:64
  366.4 10.7 %divide_convert_fusion = bf16[128,16,128]{0,2,1:T(8,128)(2,1)S(1)} fusion(bf16[2048,16,128]{0,2,1:T(8,128)(2,1)} %all-gather.11.cloned.1.call-done, f32[16,128,2048]{2,1,0:T(8,128)} %get-tuple-element.23, f32[16,128]{1,0:T(8,128)S(1)} %broadcast_maximum_fusion, pred[2048]{0:T(1024)(128)(4,1)S(1)} %iota_compare_fusion, f32[128,16]{0,1:T(8,128)S(1)} %bitcast.102), kind=kOutput, calls=%fused_computation.48 | convolution fusion | flops 1091043328 | bytes 25708544 | tf_op jit(solution)/shard_map/hqk,khd->hqd/dot_general | solution.py:74
  377.1 1.0 fusion.38
  378.2 0.4 collective-permute-start.1
  378.6 12.2 %collective-permute-done.1 = bf16[128,1536]{1,0:T(8,128)(2,1)S(1)} collective-permute-done((bf16[128,1536]{1,0:T(8,128)(2,1)S(1)}, bf16[128,1536]{1,0:T(8,128)(2,1)S(1)}, u32[]{:S(2)}, u32[]{:S(2)}) %collective-permute-start.1) | collective-permute-done | bytes 393248 | tf_op jit(solution)/shard_map/ppermute | solution.py:14
  390.8 0.9 maximum_bitcast_fusion
  (64 shorter events, 0.5 us)
Async XLA Ops:
  6.5 93.4 %all-gather.5.cloned.1.call-start = ((), (), s32[]{:S(2)}) async-start(), calls=%async_computation | async-start | bytes 8912896 | tf_op jit(solution)/shard_map/all_gather | solution.py:63
  7.4 13.1 %copy-start.4 = (f32[1536]{0:T(1024)}, f32[1536]{0:T(1024)S(1)}, u32[]{:S(2)}) copy-start(f32[1536]{0:T(1024)S(1)} %get-tuple-element.9) | copy-start | bytes 18436
  7.4 13.1 %copy-start.5 = (f32[1536]{0:T(1024)}, f32[1536]{0:T(1024)S(1)}, u32[]{:S(2)}) copy-start(f32[1536]{0:T(1024)S(1)} %get-tuple-element.10) | copy-start | bytes 18436
  7.4 179.9 %copy-start.6 = (f32[1536]{0:T(1024)}, f32[1536]{0:T(1024)S(1)}, u32[]{:S(2)}) copy-start(f32[1536]{0:T(1024)S(1)} %get-tuple-element.5) | copy-start | bytes 18436
  7.4 179.9 %copy-start.8 = (f32[1536]{0:T(1024)}, f32[1536]{0:T(1024)S(1)}, u32[]{:S(2)}) copy-start(f32[1536]{0:T(1024)S(1)} %get-tuple-element.8) | copy-start | bytes 18436
  10.5 176.8 %copy-start.10 = (pred[128]{0:T(512)(128)(4,1)}, pred[128]{0:T(512)(128)(4,1)S(1)}, u32[]{:S(2)}) copy-start(pred[128]{0:T(512)(128)(4,1)S(1)} %compare_and_fusion) | copy-start | bytes 388
  10.5 10.5 %copy-start.12 = (f32[1,128]{1,0:T(1,128)S(1)}, f32[1,128]{1,0:T(1,128)}, u32[]{:S(2)}) copy-start(f32[1,128]{1,0:T(1,128)} %param.17) | copy-start | bytes 1540
  10.5 17.9 %copy-start.15 = (s32[9]{0:T(128)S(1)}, s32[9]{0:T(128)}, u32[]{:S(2)}) copy-start(s32[9]{0:T(128)} %param.11) | copy-start | bytes 112
  10.6 19.1 %copy-start.13 = (f32[1,128]{1,0:T(1,128)S(1)}, f32[1,128]{1,0:T(1,128)}, u32[]{:S(2)}) copy-start(f32[1,128]{1,0:T(1,128)} %param.16) | copy-start | bytes 1540
  23.4 153.2 %all-gather.7.cloned.1.call-start = ((), (), s32[]{:S(2)}) async-start(), calls=%async_computation.1 | async-start | bytes 8912896 | tf_op jit(solution)/shard_map/all_gather | solution.py:64
  26.4 263.5 %all-gather.9.cloned.1.call-start = ((), (), s32[]{:S(2)}) async-start(), calls=%async_computation.2 | async-start | bytes 8912896 | tf_op jit(solution)/shard_map/all_gather | solution.py:63
  112.1 75.3 %slice-start = ((s8[6291456]{0:T(1024)(128)(4,1)}), s8[2097152]{0:T(1024)(128)(4,1)S(1)}, s32[]{:S(2)}) async-start(s8[6291456]{0:T(1024)(128)(4,1)} %bitcast.87), calls=%async_computation.4 | async-start | bytes 4194304
  176.6 10.8 %slice-start.1 = ((s8[6291456]{0:T(1024)(128)(4,1)}), s8[4194304]{0:T(1024)(128)(4,1)S(1)}, s32[]{:S(2)}) async-start(s8[6291456]{0:T(1024)(128)(4,1)} %bitcast.87), calls=%async_computation.5 | async-start | bytes 8388608
  176.6 10.8 %copy-start = (bf16[1,128,1536]{2,1,0:T(8,128)(2,1)S(1)}, bf16[1,128,1536]{2,1,0:T(8,128)(2,1)}, u32[]{:S(2)}) copy-start(bf16[1,128,1536]{2,1,0:T(8,128)(2,1)} %param.9) | copy-start | bytes 1179652
  176.6 24.6 %copy-start.3 = (bf16[128,1536]{1,0:T(8,128)(2,1)S(1)}, bf16[128,1536]{1,0:T(8,128)(2,1)}, u32[]{:S(2)}) copy-start(bf16[128,1536]{1,0:T(8,128)(2,1)} %param.10) | copy-start | bytes 1179652
  188.5 12.8 %collective-permute-start = (bf16[128,1536]{1,0:T(8,128)(2,1)S(1)}, bf16[128,1536]{1,0:T(8,128)(2,1)S(1)}, u32[]{:S(2)}, u32[]{:S(2)}) collective-permute-start(bf16[128,1536]{1,0:T(8,128)(2,1)S(1)} %fusion.41), channel_id=1, source_target_pairs={{0,16},{16,32},{32,48},{48,64},{64,80},{80,96},{96,112},{112,0},{1... | collective-permute-start | bytes 1179656 | tf_op jit(solution)/shard_map/ppermute | solution.py:14
  201.2 0.8 copy-start.1
  210.0 15.9 %copy-start.14 = (f32[1,128]{1,0:T(1,128)S(1)}, f32[1,128]{1,0:T(1,128)}, u32[]{:S(2)}) copy-start(f32[1,128]{1,0:T(1,128)} %param.16) | copy-start | bytes 1540
  220.4 145.9 %all-gather.11.cloned.1.call-start = ((), (), s32[]{:S(2)}) async-start(), calls=%async_computation.3 | async-start | bytes 8912896 | tf_op jit(solution)/shard_map/all_gather | solution.py:64
  302.0 75.1 %slice-start.2 = ((s8[6291456]{0:T(1024)(128)(4,1)}), s8[2097152]{0:T(1024)(128)(4,1)S(1)}, s32[]{:S(2)}) async-start(s8[6291456]{0:T(1024)(128)(4,1)} %bitcast.89), calls=%async_computation.6 | async-start | bytes 4194304
  366.3 10.8 %slice-start.3 = ((s8[6291456]{0:T(1024)(128)(4,1)}), s8[4194304]{0:T(1024)(128)(4,1)S(1)}, s32[]{:S(2)}) async-start(s8[6291456]{0:T(1024)(128)(4,1)} %bitcast.89), calls=%async_computation.7 | async-start | bytes 8388608
  366.3 10.8 %copy-start.7 = (f32[1536]{0:T(1024)S(1)}, f32[1536]{0:T(1024)}, u32[]{:S(2)}) copy-start(f32[1536]{0:T(1024)} %copy-done.6) | copy-start | bytes 18436
  366.3 10.8 %copy-start.9 = (f32[1536]{0:T(1024)S(1)}, f32[1536]{0:T(1024)}, u32[]{:S(2)}) copy-start(f32[1536]{0:T(1024)} %copy-done.8) | copy-start | bytes 18436
  366.3 10.8 %copy-start.11 = (pred[128]{0:T(512)(128)(4,1)S(1)}, pred[128]{0:T(512)(128)(4,1)}, u32[]{:S(2)}) copy-start(pred[128]{0:T(512)(128)(4,1)} %copy-done.10) | copy-start | bytes 388
  366.4 24.4 %copy-start.2 = (bf16[128,1536]{1,0:T(8,128)(2,1)S(1)}, bf16[128,1536]{1,0:T(8,128)(2,1)}, u32[]{:S(2)}) copy-start(bf16[128,1536]{1,0:T(8,128)(2,1)} %copy-done.1) | copy-start | bytes 1179652
  378.2 12.6 %collective-permute-start.1 = (bf16[128,1536]{1,0:T(8,128)(2,1)S(1)}, bf16[128,1536]{1,0:T(8,128)(2,1)S(1)}, u32[]{:S(2)}, u32[]{:S(2)}) collective-permute-start(bf16[128,1536]{1,0:T(8,128)(2,1)S(1)} %fusion.38), channel_id=1, source_target_pairs={{0,16},{16,32},{32,48},{48,64},{64,80},{80,96},{96,112},{112,0},{1... | collective-permute-start | bytes 1179656 | tf_op jit(solution)/shard_map/ppermute | solution.py:14
Sparse Core Ops, SparseCore 0:
  23.5 76.4 all-gather.4
  102.3 74.2 all-gather.6
  220.5 69.2 all-gather.8
  292.1 74.2 all-gather.10
where the time goes:
time: 399 us; the launch traced here: 398 us
  waiting for transfers between devices  271 us (68%)
  matrix products  64 us (16%)
  other arithmetic  27.4 us (7%)
  local copies, waits for them, and re-layouts  19.3 us (5%)
  between operations  15.4 us (4%)
    all_gather x2, waiting for transfers between devices, run_block(): key_piece = lax.all_gather(key_heads, 'seq', axis=0, tiled=True)  134 us
    all_gather x2, waiting for transfers between devices, run_block(): value_piece = lax.all_gather(value_heads, 'seq', axis=0, tiled=True)  113 us
    ppermute x2, waiting for transfers between devices, from_behind(): return lax.ppermute(value, axis, pairs)  24.5 us
    dot_general x2, matrix products, run_block(): jnp.einsum('qhd,khd->hqk', query_heads, key_piece, preferred_element_type...  24.3 us
    dot_general x2, matrix products, run_block(): jnp.einsum('hqk,khd->hqd', weights.astype(jnp.bfloat16), value_piece, pre...  21.5 us
    dot_general x2, matrix products, run_block(): projected = jnp.dot(mixed_in, w_qkv[0], preferred_element_type=jnp.float32)  16.2 us
    reduce_sum x2, other arithmetic, run_block(): denom = jnp.sum(weights, axis=-1)  15.8 us
  transfers between devices with their start and end apart: 6, of which 6 were waited for; matrix products, arithmetic and copies ran while one was open for 13% of the time, Pallas kernels for 0%

commit v1 on v0

--- a/solution.py
+++ b/solution.py
@@ -60,7 +60,9 @@
         )
         key_limit = text_start + text_live
         row_top = jnp.full((head_count, tok_rows), -1e30, jnp.float32)
-        key_piece = lax.all_gather(key_heads, "seq", axis=0, tiled=True)
+        key_piece = jnp.concatenate(
+            lax.all_to_all(jnp.stack([key_heads] * lax.axis_size("seq")), "seq", 0, 0), axis=0
+        )
         value_piece = lax.all_gather(value_heads, "seq", axis=0, tiled=True)
         scores = (
             jnp.einsum("qhd,khd->hqk", query_heads, key_piece, preferred_element_type=jnp.float32)

time: 399 us -> 415 us (1.040)
  local copies, waits for them, and re-layouts: 19.3 us -> 43.5 us
  waiting for transfers between devices: 271 us -> 250 us
  starting transfers between devices: 1.03 us -> 16.6 us
  other arithmetic: 27.4 us -> 23.1 us
    all_to_all x0 -> x2, waiting for transfers between devices: none -> 228 us  [run_block(): lax.all_to_all(jnp.stack([key_heads] * lax.axis_size('seq')), 'seq', 0, 0)]
    all_gather x2 -> x0, waiting for transfers between devices: 134 us -> none  [run_block(): key_piece = lax.all_gather(key_heads, 'seq', axis=0, tiled=True)]
    all_gather x2, waiting for transfers between devices: 113 us -> 0.04 us  [run_block(): value_piece = lax.all_gather(value_heads, 'seq', axis=0, tiled=True)]
    all_to_all x0 -> x2, local copies, waits for them, and re-layouts: none -> 20.9 us  [run_block(): lax.all_to_all(jnp.stack([key_heads] * lax.axis_size('seq')), 'seq', 0, 0)]
    all_to_all x0 -> x2, starting transfers between devices: none -> 15.5 us  [run_block(): lax.all_to_all(jnp.stack([key_heads] * lax.axis_size('seq')), 'seq', 0, 0)]
    another operation x0 -> x2, local copies, waits for them, and re-layouts: none -> 10.8 us  [run_block(): jnp.stack([key_heads] * lax.axis_size('seq'))]
  transfers between devices with their start and end apart: 6 -> 6, of which waited for: 6 -> 4; matrix products, arithmetic and copies ran while one was open for 13% -> 19% of each run, Pallas kernels for 0% -> 0%
where the time goes in v1:
time: 415 us; the launch traced here: 412 us
  waiting for transfers between devices  250 us (60%)
  matrix products  63.3 us (15%)
  local copies, waits for them, and re-layouts  43.5 us (10%)
  other arithmetic  23.1 us (6%)
  starting transfers between devices  16.6 us (4%)
  between operations  15.9 us (4%)
    all_to_all x2, waiting for transfers between devices, run_block(): lax.all_to_all(jnp.stack([key_heads] * lax.axis_size('seq')), 'seq', 0, 0)  228 us
    dot_general x2, matrix products, run_block(): jnp.einsum('qhd,khd->hqk', query_heads, key_piece, preferred_element_type...  23.5 us
    ppermute x2, waiting for transfers between devices, from_behind(): return lax.ppermute(value, axis, pairs)  22 us
    dot_general x2, matrix products, run_block(): jnp.einsum('hqk,khd->hqd', weights.astype(jnp.bfloat16), value_piece, pre...  21.5 us
    all_to_all x2, local copies, waits for them, and re-layouts, run_block(): lax.all_to_all(jnp.stack([key_heads] * lax.axis_size('seq')), 'seq', 0, 0)  20.9 us
    dot_general x2, matrix products, run_block(): projected = jnp.dot(mixed_in, w_qkv[0], preferred_element_type=jnp.float32)  16.2 us
    reduce_sum x2, other arithmetic, run_block(): denom = jnp.sum(weights, axis=-1)  15.8 us
    all_to_all x2, starting transfers between devices, run_block(): lax.all_to_all(jnp.stack([key_heads] * lax.axis_size('seq')), 'seq', 0, 0)  15.5 us
  transfers between devices with their start and end apart: 6, of which 4 were waited for; matrix products, arithmetic and copies ran while one was open for 19% of the time, Pallas kernels for 0%

profile of v1, /device:TPU:1, one launch (start us, length us, event | category | flops | bytes accessed | tf_op | source)
XLA Modules:
  0.0 412.2 jit_solution(4787157469805798683)
XLA Ops:
  6.5 0.9 slice_reduce_fusion.5
  8.1 1.1 convert_reduce_fusion.1
  9.2 1.2 fusion.62
  10.5 8.1 %fusion.2 = f32[128,6144]{1,0:T(8,128)S(1)} fusion(bf16[1,1536,6144]{2,1,0:T(8,128)(2,1)} %param.14, bf16[1,128,1536]{2,1,0:T(8,128)(2,1)} %param.9, f32[1536]{0:T(1024)S(1)} %get-tuple-element.9, f32[1536]{0:T(1024)S(1)} %get-tuple-element.10, f32[1536]{0:T(1024)S(1)} %get-tuple-element.6, f32[1536]{0:T(1024)S(1)} %get-tuple-element.7, ...), kind=kOutput, calls=%fused_computation.2 | convolution fusion | flops 2417688576 | bytes 22439040 | tf_op jit(solution)/shard_map/dot_general | solution.py:51
  18.7 0.9 slice.75
  19.6 2.0 copy.45
  21.6 1.2 slice_bitcast_fusion.3
  22.9 0.2 copy.48
  23.1 0.3 multiply_reduce_fusion.2
  23.6 0.3 multiply_convert_fusion.2
  24.1 5.4 %stack.10 = bf16[16,128,16,128]{3,1,2,0:T(8,128)(2,1)} broadcast(bf16[128,16,128]{2,0,1:T(8,128)(2,1)S(1)} %copy.32), dimensions={1,2,3} | broadcast | bytes 8912896 | tf_op jit(solution)/shard_map/stack | solution.py:64
  29.6 9.3 %all-to-all-start = ((bf16[16,128,16,128]{3,1,2,0:T(8,128)(2,1)}), bf16[16,128,16,128]{3,1,2,0:T(8,128)(2,1)}, u32[]{:S(2)}, u32[]{:S(2)}) async-start(bf16[16,128,16,128]{3,1,2,0:T(8,128)(2,1)} %stack.10), calls=%async_computation | async-start | bytes 16777216 | tf_op jit(solution)/shard_map/all_to_all | solution.py:64
  38.8 0.2 all-gather.5.cloned.1.call-start
  39.1 0.2 copy.47
  39.3 0.3 multiply_reduce_fusion.3
  39.8 0.6 fusion.96
  41.1 0.3 multiply_convert_fusion.3
  41.5 118.5 %all-to-all-done = bf16[16,128,16,128]{3,1,2,0:T(8,128)(2,1)} async-done(((bf16[16,128,16,128]{3,1,2,0:T(8,128)(2,1)}), bf16[16,128,16,128]{3,1,2,0:T(8,128)(2,1)}, u32[]{:S(2)}, u32[]{:S(2)}) %all-to-all-start) | async-done | bytes 8388640 | tf_op jit(solution)/shard_map/all_to_all | solution.py:64
  159.9 10.5 %copy.33 = bf16[16,128,16,128]{3,1,0,2:T(8,128)(2,1)} copy(bf16[16,128,16,128]{3,1,2,0:T(8,128)(2,1)} %all-to-all-done) | data formatting | bytes 16777216 | tf_op jit(solution)/shard_map/all_to_all | solution.py:64
  170.5 11.8 %fusion.4 = (f32[16,128]{1,0:T(8,128)S(1)}, f32[16,128,2048]{2,1,0:T(8,128)}) fusion(pred[2048]{0:T(1024)(128)(4,1)S(1)} %iota_compare_fusion.1, bf16[2048,16,128]{2,0,1:T(8,128)(2,1)} %bitcast.84, bf16[128,16,128]{2,1,0:T(8,128)(2,1)S(1)} %multiply_convert_fusion.3), kind=kOutput, calls=%fused_computation.8 | convolution fusion | flops 1086322688 | bytes 25700352 | tf_op jit(solution)/shard_map/qhd,khd->hqk/dot_general | solution.py:68
  182.2 7.9 %fusion.6 = f32[16,128]{1,0:T(8,128)S(1)} fusion(f32[16,128,2048]{2,1,0:T(8,128)} %get-tuple-element.20, f32[16,128]{1,0:T(8,128)S(1)} %broadcast_maximum_fusion.1, pred[2048]{0:T(1024)(128)(4,1)S(1)} %iota_compare_fusion.1), kind=kLoop, calls=%fused_computation.10 | loop fusion | flops 16775168 | bytes 16795648 | tf_op jit(solution)/shard_map/reduce_sum | solution.py:75
  190.2 10.7 %divide_convert_fusion.1 = bf16[128,16,128]{0,2,1:T(8,128)(2,1)S(1)} fusion(bf16[2048,16,128]{0,2,1:T(8,128)(2,1)} %all-gather.3.cloned.1.call-done, f32[16,128,2048]{2,1,0:T(8,128)} %get-tuple-element.20, f32[16,128]{1,0:T(8,128)S(1)} %broadcast_maximum_fusion.1, pred[2048]{0:T(1024)(128)(4,1)S(1)} %iota_compare_fusion.1, f32[128,16]{0,1:T(8,128)S(1)} %bitcast.100), kind=kOutput, calls=%fused_computation.52 | convolution fusion | flops 1091043328 | bytes 25708544 | tf_op jit(solution)/shard_map/hqk,khd->hqd/dot_general | solution.py:76
  201.0 1.0 fusion.41
  202.0 0.8 collective-permute-start
  202.9 11.4 %collective-permute-done = bf16[128,1536]{1,0:T(8,128)(2,1)S(1)} collective-permute-done((bf16[128,1536]{1,0:T(8,128)(2,1)S(1)}, bf16[128,1536]{1,0:T(8,128)(2,1)S(1)}, u32[]{:S(2)}, u32[]{:S(2)}) %collective-permute-start) | collective-permute-done | bytes 393248 | tf_op jit(solution)/shard_map/ppermute | solution.py:14
  214.2 0.2 convert_reduce_fusion
  214.4 0.3 fusion.57
  214.7 0.3 copy-done.3
  215.0 8.1 %fusion = f32[128,6144]{1,0:T(8,128)S(1)} fusion(bf16[1,1536,6144]{2,1,0:T(8,128)(2,1)} %param.14, bf16[128,1536]{1,0:T(8,128)(2,1)S(1)} %get-tuple-element.12, f32[1536]{0:T(1024)} %copy-done.6, f32[1536]{0:T(1024)} %copy-done.7, f32[1536]{0:T(1024)S(1)} %get-tuple-element.6, f32[1536]{0:T(1024)S(1)} %get-tuple-element.7, f32[128]{0:T(128)S(1)} %add_rsqrt_fusion.4, ...), kind=kOutput, calls=%fused_computation | convolution fusion | flops 2417688576 | bytes 22439040 | tf_op jit(solution)/shard_map/dot_general | solution.py:51
  223.1 0.9 slice.74
  223.9 2.0 copy.46
  226.0 1.2 slice_bitcast_fusion.1
  227.2 0.2 copy.50
  227.4 0.3 multiply_reduce_fusion
  228.0 1.0 multiply_convert_fusion
  229.1 5.3 %stack.12 = bf16[16,128,16,128]{3,1,2,0:T(8,128)(2,1)} broadcast(bf16[128,16,128]{2,0,1:T(8,128)(2,1)S(1)} %copy.40), dimensions={1,2,3} | broadcast | bytes 8912896 | tf_op jit(solution)/shard_map/stack | solution.py:64
  234.5 6.3 %all-to-all-start.1 = ((bf16[16,128,16,128]{3,1,2,0:T(8,128)(2,1)}), bf16[16,128,16,128]{3,1,2,0:T(8,128)(2,1)}, u32[]{:S(2)}, u32[]{:S(2)}) async-start(bf16[16,128,16,128]{3,1,2,0:T(8,128)(2,1)} %stack.12), calls=%async_computation.1 | async-start | bytes 16777216 | tf_op jit(solution)/shard_map/all_to_all | solution.py:64
  241.3 0.2 copy.49
  241.5 0.3 multiply_reduce_fusion.1
  242.1 0.3 multiply_convert_fusion.1
  242.4 109.3 %all-to-all-done.1 = bf16[16,128,16,128]{3,1,2,0:T(8,128)(2,1)} async-done(((bf16[16,128,16,128]{3,1,2,0:T(8,128)(2,1)}), bf16[16,128,16,128]{3,1,2,0:T(8,128)(2,1)}, u32[]{:S(2)}, u32[]{:S(2)}) %all-to-all-start.1) | async-done | bytes 8388640 | tf_op jit(solution)/shard_map/all_to_all | solution.py:64
  351.7 10.3 %copy.41 = bf16[16,128,16,128]{3,1,0,2:T(8,128)(2,1)} copy(bf16[16,128,16,128]{3,1,2,0:T(8,128)(2,1)} %all-to-all-done.1) | data formatting | bytes 16777216 | tf_op jit(solution)/shard_map/all_to_all | solution.py:64
  362.1 11.8 %fusion.5 = (f32[16,128]{1,0:T(8,128)S(1)}, f32[16,128,2048]{2,1,0:T(8,128)}) fusion(pred[2048]{0:T(1024)(128)(4,1)S(1)} %iota_compare_fusion, bf16[2048,16,128]{2,0,1:T(8,128)(2,1)} %bitcast.85, bf16[128,16,128]{2,1,0:T(8,128)(2,1)S(1)} %multiply_convert_fusion.1), kind=kOutput, calls=%fused_computation.9 | convolution fusion | flops 1086322688 | bytes 25700352 | tf_op jit(solution)/shard_map/qhd,khd->hqk/dot_general | solution.py:68
  373.9 7.9 %fusion.8 = f32[16,128]{1,0:T(8,128)S(1)} fusion(f32[16,128,2048]{2,1,0:T(8,128)} %get-tuple-element.22, f32[16,128]{1,0:T(8,128)S(1)} %broadcast_maximum_fusion, pred[2048]{0:T(1024)(128)(4,1)S(1)} %iota_compare_fusion), kind=kLoop, calls=%fused_computation.12 | loop fusion | flops 16775168 | bytes 16795648 | tf_op jit(solution)/shard_map/reduce_sum | solution.py:75
  381.9 10.7 %divide_convert_fusion = bf16[128,16,128]{0,2,1:T(8,128)(2,1)S(1)} fusion(bf16[2048,16,128]{0,2,1:T(8,128)(2,1)} %all-gather.5.cloned.1.call-done, f32[16,128,2048]{2,1,0:T(8,128)} %get-tuple-element.22, f32[16,128]{1,0:T(8,128)S(1)} %broadcast_maximum_fusion, pred[2048]{0:T(1024)(128)(4,1)S(1)} %iota_compare_fusion, f32[128,16]{0,1:T(8,128)S(1)} %bitcast.101), kind=kOutput, calls=%fused_computation.47 | convolution fusion | flops 1091043328 | bytes 25708544 | tf_op jit(solution)/shard_map/hqk,khd->hqd/dot_general | solution.py:76
  392.7 1.0 fusion.38
  393.8 10.6 %collective-permute-done.1 = bf16[128,1536]{1,0:T(8,128)(2,1)S(1)} collective-permute-done((bf16[128,1536]{1,0:T(8,128)(2,1)S(1)}, bf16[128,1536]{1,0:T(8,128)(2,1)S(1)}, u32[]{:S(2)}, u32[]{:S(2)}) %collective-permute-start.1) | collective-permute-done | bytes 393248 | tf_op jit(solution)/shard_map/ppermute | solution.py:14
  404.4 0.9 maximum_bitcast_fusion
  (74 shorter events, 1.3 us)
Async XLA Ops:
  6.5 183.6 %all-gather.3.cloned.1.call-start = ((), (), s32[]{:S(2)}) async-start(), calls=%async_computation.2 | async-start | bytes 8912896 | tf_op jit(solution)/shard_map/all_gather | solution.py:66
  7.4 15.6 %copy-start.6 = (f32[1536]{0:T(1024)}, f32[1536]{0:T(1024)S(1)}, u32[]{:S(2)}) copy-start(f32[1536]{0:T(1024)S(1)} %get-tuple-element.9) | copy-start | bytes 18436
  7.4 15.6 %copy-start.7 = (f32[1536]{0:T(1024)}, f32[1536]{0:T(1024)S(1)}, u32[]{:S(2)}) copy-start(f32[1536]{0:T(1024)S(1)} %get-tuple-element.10) | copy-start | bytes 18436
  7.4 193.5 %copy-start.8 = (f32[1536]{0:T(1024)}, f32[1536]{0:T(1024)S(1)}, u32[]{:S(2)}) copy-start(f32[1536]{0:T(1024)S(1)} %get-tuple-element.5) | copy-start | bytes 18436
  7.4 193.5 %copy-start.10 = (f32[1536]{0:T(1024)}, f32[1536]{0:T(1024)S(1)}, u32[]{:S(2)}) copy-start(f32[1536]{0:T(1024)S(1)} %get-tuple-element.8) | copy-start | bytes 18436
  10.5 190.4 %copy-start.12 = (pred[128]{0:T(512)(128)(4,1)}, pred[128]{0:T(512)(128)(4,1)S(1)}, u32[]{:S(2)}) copy-start(pred[128]{0:T(512)(128)(4,1)S(1)} %compare_and_fusion) | copy-start | bytes 388
  10.5 13.1 %copy-start.14 = (f32[1,128]{1,0:T(1,128)S(1)}, f32[1,128]{1,0:T(1,128)}, u32[]{:S(2)}) copy-start(f32[1,128]{1,0:T(1,128)} %param.17) | copy-start | bytes 1540
  22.9 16.2 %copy-start.1 = (f32[16,8,16,128]{3,1,2,0:T(8,128)S(1)}, f32[16,8,16,128]{3,1,2,0:T(8,128)}, u32[]{:S(2)}) copy-start(f32[16,8,16,128]{3,1,2,0:T(8,128)} %get-tuple-element.15) | copy-start | bytes 3145732
  23.1 16.8 %copy-start.17 = (s32[9]{0:T(128)S(1)}, s32[9]{0:T(128)}, u32[]{:S(2)}) copy-start(s32[9]{0:T(128)} %param.11) | copy-start | bytes 112
  23.1 18.0 %copy-start.15 = (f32[1,128]{1,0:T(1,128)S(1)}, f32[1,128]{1,0:T(1,128)}, u32[]{:S(2)}) copy-start(f32[1,128]{1,0:T(1,128)} %param.16) | copy-start | bytes 1540
  29.6 130.4 %all-to-all-start = ((bf16[16,128,16,128]{3,1,2,0:T(8,128)(2,1)}), bf16[16,128,16,128]{3,1,2,0:T(8,128)(2,1)}, u32[]{:S(2)}, u32[]{:S(2)}) async-start(bf16[16,128,16,128]{3,1,2,0:T(8,128)(2,1)} %stack.10), calls=%async_computation | async-start | bytes 16777216 | tf_op jit(solution)/shard_map/all_to_all | solution.py:64
  38.8 343.0 %all-gather.5.cloned.1.call-start = ((), (), s32[]{:S(2)}) async-start(), calls=%async_computation.3 | async-start | bytes 8912896 | tf_op jit(solution)/shard_map/all_gather | solution.py:66
  182.2 18.8 %slice-start = ((s8[6291456]{0:T(1024)(128)(4,1)}), s8[2097152]{0:T(1024)(128)(4,1)S(1)}, s32[]{:S(2)}) async-start(s8[6291456]{0:T(1024)(128)(4,1)} %bitcast.86), calls=%async_computation.4 | async-start | bytes 4194304
  190.2 10.8 %slice-start.1 = ((s8[6291456]{0:T(1024)(128)(4,1)}), s8[4194304]{0:T(1024)(128)(4,1)S(1)}, s32[]{:S(2)}) async-start(s8[6291456]{0:T(1024)(128)(4,1)} %bitcast.86), calls=%async_computation.5 | async-start | bytes 8388608
  190.2 10.8 %copy-start = (bf16[1,128,1536]{2,1,0:T(8,128)(2,1)S(1)}, bf16[1,128,1536]{2,1,0:T(8,128)(2,1)}, u32[]{:S(2)}) copy-start(bf16[1,128,1536]{2,1,0:T(8,128)(2,1)} %param.9) | copy-start | bytes 1179652
  190.2 24.1 %copy-start.5 = (bf16[128,1536]{1,0:T(8,128)(2,1)S(1)}, bf16[128,1536]{1,0:T(8,128)(2,1)}, u32[]{:S(2)}) copy-start(bf16[128,1536]{1,0:T(8,128)(2,1)} %param.10) | copy-start | bytes 1179652
  202.0 12.2 %collective-permute-start = (bf16[128,1536]{1,0:T(8,128)(2,1)S(1)}, bf16[128,1536]{1,0:T(8,128)(2,1)S(1)}, u32[]{:S(2)}, u32[]{:S(2)}) collective-permute-start(bf16[128,1536]{1,0:T(8,128)(2,1)S(1)} %fusion.41), channel_id=1, source_target_pairs={{0,16},{16,32},{32,48},{48,64},{64,80},{80,96},{96,112},{112,0},{1... | collective-permute-start | bytes 1179656 | tf_op jit(solution)/shard_map/ppermute | solution.py:14
  214.2 0.8 copy-start.3
  227.2 14.1 %copy-start.2 = (f32[16,8,16,128]{3,1,2,0:T(8,128)S(1)}, f32[16,8,16,128]{3,1,2,0:T(8,128)}, u32[]{:S(2)}) copy-start(f32[16,8,16,128]{3,1,2,0:T(8,128)} %get-tuple-element.13) | copy-start | bytes 3145732
  227.4 14.6 %copy-start.16 = (f32[1,128]{1,0:T(1,128)S(1)}, f32[1,128]{1,0:T(1,128)}, u32[]{:S(2)}) copy-start(f32[1,128]{1,0:T(1,128)} %param.16) | copy-start | bytes 1540
  234.5 117.3 %all-to-all-start.1 = ((bf16[16,128,16,128]{3,1,2,0:T(8,128)(2,1)}), bf16[16,128,16,128]{3,1,2,0:T(8,128)(2,1)}, u32[]{:S(2)}, u32[]{:S(2)}) async-start(bf16[16,128,16,128]{3,1,2,0:T(8,128)(2,1)} %stack.12), calls=%async_computation.1 | async-start | bytes 16777216 | tf_op jit(solution)/shard_map/all_to_all | solution.py:64
  373.9 18.7 %slice-start.2 = ((s8[6291456]{0:T(1024)(128)(4,1)}), s8[2097152]{0:T(1024)(128)(4,1)S(1)}, s32[]{:S(2)}) async-start(s8[6291456]{0:T(1024)(128)(4,1)} %bitcast.88), calls=%async_computation.6 | async-start | bytes 4194304
  381.8 10.8 %slice-start.3 = ((s8[6291456]{0:T(1024)(128)(4,1)}), s8[4194304]{0:T(1024)(128)(4,1)S(1)}, s32[]{:S(2)}) async-start(s8[6291456]{0:T(1024)(128)(4,1)} %bitcast.88), calls=%async_computation.7 | async-start | bytes 8388608
  381.8 10.8 %copy-start.9 = (f32[1536]{0:T(1024)S(1)}, f32[1536]{0:T(1024)}, u32[]{:S(2)}) copy-start(f32[1536]{0:T(1024)} %copy-done.8) | copy-start | bytes 18436
  381.8 10.8 %copy-start.11 = (f32[1536]{0:T(1024)S(1)}, f32[1536]{0:T(1024)}, u32[]{:S(2)}) copy-start(f32[1536]{0:T(1024)} %copy-done.10) | copy-start | bytes 18436
  381.8 10.8 %copy-start.13 = (pred[128]{0:T(512)(128)(4,1)S(1)}, pred[128]{0:T(512)(128)(4,1)}, u32[]{:S(2)}) copy-start(pred[128]{0:T(512)(128)(4,1)} %copy-done.12) | copy-start | bytes 388
  381.8 22.6 %copy-start.4 = (bf16[128,1536]{1,0:T(8,128)(2,1)S(1)}, bf16[128,1536]{1,0:T(8,128)(2,1)}, u32[]{:S(2)}) copy-start(bf16[128,1536]{1,0:T(8,128)(2,1)} %copy-done.3) | copy-start | bytes 1179652
  393.7 10.7 %collective-permute-start.1 = (bf16[128,1536]{1,0:T(8,128)(2,1)S(1)}, bf16[128,1536]{1,0:T(8,128)(2,1)S(1)}, u32[]{:S(2)}, u32[]{:S(2)}) collective-permute-start(bf16[128,1536]{1,0:T(8,128)(2,1)S(1)} %fusion.38), channel_id=1, source_target_pairs={{0,16},{16,32},{32,48},{48,64},{64,80},{80,96},{96,112},{112,0},{1... | collective-permute-start | bytes 1179656 | tf_op jit(solution)/shard_map/ppermute | solution.py:14
Sparse Core Ops, SparseCore 0:
  21.7 150.0 all-gather.2
  226.1 145.7 all-gather.4
